TPU v7x, 32 devices: a whole 2x2x4 slice. The times are simulated.
32 devices in a mesh: tm: 4 (over x, core), chan: 8 (over z, y).
Axes of the slice: x: 2, y: 2, z: 4, core: 2. Of those that a mesh axis runs over, the one named last changes fastest.
Arguments:
- raw_blocks: bfloat16 [16, 5120, 1024], P('tm', 'chan'), may hold values from -6 to 6
- fir_taps: bfloat16 [128], replicated, may hold values from -0.5 to 0.5
- recorder_channel: int32 [5120], replicated, may hold values from 0 to 5119, as said below
- pairs: int32 [4096, 2], P('chan'), may hold values from 0 to 5119, as said below
Outputs:
- stacks: float32 [4096, 256], P('chan')
Inputs may be any that keep to these rules, and one draw needn't show every extreme that they name: `recorder_channel`: A permutation of the channels; each aligned block of 640 recorder rows holds exactly 80 channels of every range of 640 consecutive channels. `pairs`: each aligned block of 512 rows names exactly 32 distinct channels of every range of 640 consecutive channels.
All inputs are finite; a program needn't handle non-finite values.
Results may differ from a plain program's by a relative error of at most 0.0084.
Values may be sent and summed in bfloat16 or wider, within the bound.
No kernel may reach another device: no remote copies, remote signals or barrier semaphores. Data moves between devices by JAX's collectives and lax.ppermute only.
A program may use at most 128 MiB of HBM per device.

v0:
```python
import jax
import jax.numpy as jnp
from jax import lax
from jax.sharding import PartitionSpec as P

NB = 128
SMOOTH = 4


def make_fir(fir_taps, length):
    taps_n = fir_taps.shape[0]
    period = taps_n + length
    padded = jnp.concatenate([fir_taps.astype(jnp.float32), jnp.zeros((length,), jnp.float32)])
    repeated = jnp.tile(padded, length)[: length * (period - 1)].reshape(length, period - 1)[
        :, :length
    ]
    return repeated.astype(jnp.bfloat16)


def make_table(length, bin_count):
    samples = jnp.arange(length, dtype=jnp.int32)
    freqs = jnp.arange(1, bin_count + 1, dtype=jnp.int32)
    phase_idx = samples[:, None] * freqs[None, :] % length
    angles = phase_idx.astype(jnp.float32) * (2.0 * jnp.pi / length)
    return jnp.concatenate([jnp.cos(angles), -jnp.sin(angles)], axis=1).astype(jnp.bfloat16)


def make_smooth(bin_count, half_width):
    places = jnp.arange(bin_count, dtype=jnp.int32)
    band_mask = (jnp.abs(places[:, None] - places[None, :]) <= half_width).astype(jnp.float32)
    return band_mask / jnp.sum(band_mask, axis=0, keepdims=True)


def whiten(spectrum, smoother):
    bin_count = spectrum.shape[-1] // 2
    real_part = spectrum[..., :bin_count]
    imag_part = spectrum[..., bin_count:]
    magnitude = jnp.sqrt(real_part * real_part + imag_part * imag_part)
    smoothed = jnp.dot(magnitude, smoother, precision=lax.Precision.HIGHEST)
    mean_level = jnp.mean(magnitude, axis=-1, keepdims=True)
    divisor = smoothed + 0.1 * mean_level + 1e-06
    return (spectrum / jnp.concatenate([divisor, divisor], axis=-1)).astype(jnp.bfloat16)


def cross(left_rows, right_rows):
    bin_count = left_rows.shape[-1] // 2
    left_f = left_rows.astype(jnp.float32)
    right_f = right_rows.astype(jnp.float32)
    left_re, left_im = (left_f[..., :bin_count], left_f[..., bin_count:])
    right_re, right_im = (right_f[..., :bin_count], right_f[..., bin_count:])
    real_out = left_re * right_re + left_im * right_im
    imag_out = left_im * right_re - left_re * right_im
    return jnp.concatenate([real_out, imag_out], axis=-1)


def local(raw_blocks, fir_taps, recorder_channel, pairs):
    windows, ch_dev, length = raw_blocks.shape
    rows_of = jnp.argsort(recorder_channel, stable=True)
    endpoints = jnp.concatenate([pairs[:, 0], pairs[:, 1]])
    wanted_ids = jnp.take(rows_of, endpoints)
    fir_matrix = make_fir(fir_taps, length)
    dft_table = make_table(length, NB)
    smoother = make_smooth(NB, SMOOTH)
    flat_rows = raw_blocks.reshape(windows * ch_dev, length)
    filtered = jnp.dot(flat_rows, fir_matrix, preferred_element_type=jnp.float32).astype(
        jnp.bfloat16
    )
    spectrum = jnp.dot(filtered, dft_table, preferred_element_type=jnp.float32)
    whitened = whiten(spectrum, smoother).reshape(windows, ch_dev, 2 * NB)
    pair_count = pairs.shape[0]
    empty = jnp.zeros((windows, 2 * pair_count, 2 * NB), jnp.bfloat16)
    part_rows = lax.all_gather(whitened, "chan", axis=1, tiled=True)
    inside = (wanted_ids >= 0) & (wanted_ids < part_rows.shape[1])
    taken = jnp.take(part_rows, jnp.clip(wanted_ids, 0, part_rows.shape[1] - 1), axis=1)
    chosen = jnp.where(inside[None, :, None], taken, empty)
    products = cross(chosen[:, :pair_count], chosen[:, pair_count:])
    stacked = jnp.sum(products, axis=0)
    summed = lax.psum(stacked, "tm")
    return summed / (windows * lax.axis_size("tm"))


def solution(mesh):
    in_specs = (P("tm", "chan", None), P(), P(), P("chan", None))
    out_specs = P("chan", None)
    return jax.shard_map(local, mesh=mesh, in_specs=in_specs, out_specs=out_specs, check_vma=False)
```

profile of v0, /device:TPU:0, one launch (start us, length us, event | category | flops | bytes accessed | tf_op | source)
XLA Modules:
  0.0 248.1 jit_solution(11060469899976761753)
XLA Ops:
  6.5 0.0 all-gather.2.cloned.1.call-start
  6.6 2.2 cosine_convert_fusion
  8.8 0.7 concatenate.69
  9.5 0.2 tile.10
  9.7 3.8 %tile.11 = bf16[1179648]{0:T(1024)(128)(2,1)} reshape(bf16[1024,1152]{1,0:T(8,128)(2,1)S(1)} %tile.10) | data formatting | bytes 4718592 | tf_op jit(solution)/shard_map/tile | solution.py:14
  13.5 0.0 slice-start
  13.5 1.7 slice-done
  15.2 6.4 %reshape.232 = bf16[1024,1151]{1,0:T(8,128)(2,1)} reshape(bf16[1178624]{0:T(1024)(128)(2,1)S(1)} %slice-done) | data formatting | bytes 4714496 | tf_op jit(solution)/shard_map/reshape | solution.py:14
  21.5 10.3 %fusion.6 = f32[2560,256]{1,0:T(8,128)S(1)} fusion(bf16[2560,1024]{1,0:T(8,128)(2,1)} %bitcast.16, bf16[1024,1151]{1,0:T(8,128)(2,1)} %reshape.232, bf16[1024,128]{1,0:T(8,128)(2,1)S(1)} %get-tuple-element.16, bf16[1024,128]{1,0:T(8,128)(2,1)S(1)} %get-tuple-element.15), kind=kOutput, calls=%fused_computation.14 | convolution fusion | flops 6714556416 | bytes 10485760 | tf_op jit(solution)/shard_map/dot_general | solution.py:68
  31.9 0.5 fusion.17
  32.4 1.5 fusion
  33.9 0.5 fusion.1
  34.4 0.0 copy-start
  34.5 0.0 copy-start.1
  34.5 2.1 copy.11
  36.6 0.0 all-gather.2.cloned.1.call-update
  36.6 0.0 all-reduce.3.cloned.1.call-start
  36.6 0.0 copy-done
  36.6 6.8 %sort.17 = (s32[5120]{0:T(1024)}, s32[5120]{0:T(1024)S(1)}) sort(s32[5120]{0:T(1024)S(1)} %copy-done, s32[5120]{0:T(1024)S(1)} %iota.22), dimensions={0}, to_apply=%region_0.0 | sort | flops 66560 | bytes 81920 | tf_op jit(solution)/shard_map/jit(argsort)/sort | solution.py:58
  43.4 0.0 copy-done.1
  43.4 6.4 %gather_fusion = s32[1024]{0:T(1024)S(1)} fusion(s32[5120]{0:T(1024)S(1)} %get-tuple-element.6, s32[1024]{0:T(1024)S(1)} %broadcast_clamp_fusion.1), kind=kCustom, calls=%fused_computation | custom fusion | bytes 12288 | tf_op jit(solution)/shard_map/jit(_take)/gather | solution.py:60
  49.9 140.1 %all-gather.2.cloned.1.call-done = bf16[4,5120,256]{2,0,1:T(4,128)(2,1)} async-done(((bf16[4,640,256]{2,0,1:T(4,128)(2,1)}), bf16[4,5120,256]{2,0,1:T(4,128)(2,1)}) %all-gather.2.cloned.1.call-update) | async-done | bytes 10485776 | tf_op jit(solution)/shard_map/all_gather | solution.py:72
  190.0 7.9 %gather_fusion.1 = bf16[1024,4,256]{2,1,0:T(4,128)(2,1)S(1)} fusion(bf16[4,5120,256]{2,0,1:T(4,128)(2,1)} %all-gather.2.cloned.1.call-done, s32[1024]{0:T(1024)S(1)} %broadcast_clamp_fusion), kind=kCustom, calls=%fused_computation.1 | custom fusion | bytes 4198400 | tf_op jit(solution)/shard_map/jit(_take)/gather | solution.py:74
  197.9 6.5 %select_bitcast_fusion = bf16[4,1024,256]{2,0,1:T(4,128)(2,1)S(1)} fusion(bf16[1024,4,256]{2,1,0:T(4,128)(2,1)S(1)} %gather_fusion.1, pred[1024]{0:T(1024)(128)(4,1)S(1)} %get-tuple-element.12, pred[1024]{0:T(1024)(128)(4,1)S(1)} %get-tuple-element.11), kind=kLoop, calls=%fused_computation.9 | loop fusion | flops 2097152 | bytes 4196352 | tf_op jit(solution)/shard_map/jit(_where)/select_n | solution.py:75
  204.4 0.5 slice_convert_fusion.1
  204.9 0.5 multiply_add_fusion
  205.5 2.2 maximum_reduce_fusion
  207.7 0.0 all-reduce.3.cloned.1.call-update
  207.7 31.7 %all-reduce.3.cloned.1.call-done = f32[512,256]{1,0:T(8,128)} async-done(((f32[512,256]{1,0:T(8,128)}), f32[512,256]{1,0:T(8,128)}) %all-reduce.3.cloned.1.call-update) | async-done | bytes 524304 | tf_op jit(solution)/shard_map/psum | solution.py:78
  239.4 1.9 broadcast_multiply_fusion
  (10 shorter events, 0.1 us)
Async XLA Ops:
  6.5 183.4 %all-gather.2.cloned.1.call-start = ((), (), s32[]{:S(2)}) async-start(), calls=%async_computation | async-start | bytes 11796480 | tf_op jit(solution)/shard_map/all_gather | solution.py:72
  13.5 1.7 slice-start
  34.4 2.2 copy-start
  34.5 9.0 %copy-start.1 = (s32[512,2]{0,1:T(2,128)S(1)}, s32[512,2]{0,1:T(2,128)}, u32[]{:S(2)}) copy-start(s32[512,2]{0,1:T(2,128)} %param.7) | copy-start | bytes 12292
  36.6 202.8 %all-reduce.3.cloned.1.call-start = ((), (), s32[]{:S(2)}) async-start(), calls=%async_computation.1 | async-start | bytes 1048576 | tf_op jit(solution)/shard_map/psum | solution.py:78
Sparse Core Ops, SparseCore 0:
  36.7 153.2 all-gather.1
  207.8 31.5 all-reduce.2
where the time goes:
time: 248 us
  waiting for transfers between devices  172 us (69%)
  local copies, waits for them, and re-layouts  29.1 us (12%)
  other arithmetic  21.8 us (9%)
  between operations  13.5 us (5%)
  matrix products  11.8 us (5%)
    all_gather x1, waiting for transfers between devices, local(): part_rows = lax.all_gather(whitened, 'chan', axis=1, tiled=True)  140 us
    psum x1, waiting for transfers between devices, local(): summed = lax.psum(stacked, 'tm')  31.7 us
    dot_general x1, matrix products, local(): spectrum = jnp.dot(filtered, dft_table, preferred_element_type=jnp.float32)  10.3 us
    gather x1, local copies, waits for them, and re-layouts, local(): jnp.take(part_rows, jnp.clip(wanted_ids, 0, part_rows.shape[1] - 1), axis=1)  7.92 us
    sort x1, other arithmetic, local(): rows_of = jnp.argsort(recorder_channel, stable=True)  6.76 us
    select_n x1, other arithmetic, local(): chosen = jnp.where(inside[None, :, None], taken, empty)  6.46 us
    gather x1, local copies, waits for them, and re-layouts, local(): wanted_ids = jnp.take(rows_of, endpoints)  6.37 us
    reshape x1, local copies, waits for them, and re-layouts, make_fir(): jnp.tile(padded, length)[:length * (period - 1)].reshape(length, period - 1)  6.35 us
  transfers between devices with their start and end apart: 2, of which 2 were waited for; matrix products, arithmetic and copies ran while one was open for 5% of the time, Pallas kernels for 0%

commit v1 on v0

--- a/solution.py
+++ b/solution.py
@@ -2,6 +2,7 @@
 import jax.numpy as jnp
 from jax import lax
 from jax.sharding import PartitionSpec as P
+from jax.lax import all_gather
 
 NB = 128
 SMOOTH = 4
@@ -69,7 +70,7 @@
     whitened = whiten(spectrum, smoother).reshape(windows, ch_dev, 2 * NB)
     pair_count = pairs.shape[0]
     empty = jnp.zeros((windows, 2 * pair_count, 2 * NB), jnp.bfloat16)
-    part_rows = lax.all_gather(whitened, "chan", axis=1, tiled=True)
+    part_rows = jnp.concatenate(all_gather(whitened, "chan"), axis=1)
     inside = (wanted_ids >= 0) & (wanted_ids < part_rows.shape[1])
     taken = jnp.take(part_rows, jnp.clip(wanted_ids, 0, part_rows.shape[1] - 1), axis=1)
     chosen = jnp.where(inside[None, :, None], taken, empty)

time: 248 us -> 262 us (1.056)
  local copies, waits for them, and re-layouts: 29.1 us -> 41.4 us
    reshape x1, local copies, waits for them, and re-layouts: 2.09 us -> 14.6 us  [local(): part_rows = jnp.concatenate(all_gather(whitened, 'chan'), axis=1)]
where the time goes in v1:
time: 262 us
  waiting for transfers between devices  172 us (66%)
  local copies, waits for them, and re-layouts  41.4 us (16%)
  other arithmetic  23 us (9%)
  between operations  13.5 us (5%)
  matrix products  11.7 us (4%)
    all_gather x1, waiting for transfers between devices, local(): part_rows = jnp.concatenate(all_gather(whitened, 'chan'), axis=1)  140 us
    psum x1, waiting for transfers between devices, local(): summed = lax.psum(stacked, 'tm')  31.7 us
    reshape x1, local copies, waits for them, and re-layouts, local(): part_rows = jnp.concatenate(all_gather(whitened, 'chan'), axis=1)  14.6 us
    dot_general x1, matrix products, local(): spectrum = jnp.dot(filtered, dft_table, preferred_element_type=jnp.float32)  10.2 us
    gather x1, local copies, waits for them, and re-layouts, local(): jnp.take(part_rows, jnp.clip(wanted_ids, 0, part_rows.shape[1] - 1), axis=1)  7.92 us
    sort x1, other arithmetic, local(): rows_of = jnp.argsort(recorder_channel, stable=True)  6.76 us
    select_n x1, other arithmetic, local(): chosen = jnp.where(inside[None, :, None], taken, empty)  6.46 us
    reshape x1, local copies, waits for them, and re-layouts, make_fir(): jnp.tile(padded, length)[:length * (period - 1)].reshape(length, period - 1)  6.35 us
  transfers between devices with their start and end apart: 2, of which 2 were waited for; matrix products, arithmetic and copies ran while one was open for 5% of the time, Pallas kernels for 0%

profile of v1, /device:TPU:0, one launch (start us, length us, event | category | flops | bytes accessed | tf_op | source)
XLA Modules:
  0.0 261.7 jit_solution(6801155272109285621)
XLA Ops:
  6.5 0.0 all-gather.2.cloned.1.call-start
  6.6 0.7 concatenate.69
  7.2 0.2 tile.10
  7.4 3.8 %tile.11 = bf16[1179648]{0:T(1024)(128)(2,1)} reshape(bf16[1024,1152]{1,0:T(8,128)(2,1)S(1)} %tile.10) | data formatting | bytes 4718592 | tf_op jit(solution)/shard_map/tile | solution.py:15
  11.3 0.0 slice-start
  11.3 1.7 slice-done
  12.9 6.4 %reshape.235 = bf16[1024,1151]{1,0:T(8,128)(2,1)} reshape(bf16[1178624]{0:T(1024)(128)(2,1)S(1)} %slice-done) | data formatting | bytes 4714496 | tf_op jit(solution)/shard_map/reshape | solution.py:15
  19.3 2.4 cosine_convert_fusion
  21.7 10.2 %fusion.6 = f32[2560,256]{1,0:T(8,128)S(1)} fusion(bf16[2560,1024]{1,0:T(8,128)(2,1)} %bitcast.22, bf16[1024,1151]{1,0:T(8,128)(2,1)} %reshape.235, bf16[1024,128]{1,0:T(8,128)(2,1)S(1)} %get-tuple-element.16, bf16[1024,128]{1,0:T(8,128)(2,1)S(1)} %get-tuple-element.15), kind=kOutput, calls=%fused_computation.14 | convolution fusion | flops 6714556416 | bytes 10485760 | tf_op jit(solution)/shard_map/dot_general | solution.py:69
  31.8 0.5 fusion.17
  32.4 1.5 fusion
  33.9 0.0 copy-start
  33.9 0.0 copy-start.1
  33.9 1.6 fusion.1
  35.5 0.0 all-gather.2.cloned.1.call-update
  35.5 0.3 all-reduce.3.cloned.1.call-start
  35.8 0.0 copy-done
  35.8 6.8 %sort.17 = (s32[5120]{0:T(1024)}, s32[5120]{0:T(1024)S(1)}) sort(s32[5120]{0:T(1024)S(1)} %copy-done, s32[5120]{0:T(1024)S(1)} %iota.22), dimensions={0}, to_apply=%region_0.0 | sort | flops 66560 | bytes 81920 | tf_op jit(solution)/shard_map/jit(argsort)/sort | solution.py:59
  42.6 0.0 copy-done.1
  42.6 6.2 %gather_fusion = s32[1024]{0:T(1024)S(1)} fusion(s32[5120]{0:T(1024)S(1)} %get-tuple-element.6, s32[1024]{0:T(1024)S(1)} %broadcast_clamp_fusion.1), kind=kCustom, calls=%fused_computation | custom fusion | bytes 12288 | tf_op jit(solution)/shard_map/jit(_take)/gather | solution.py:61
  48.8 140.1 %all-gather.2.cloned.1.call-done = bf16[8,4,640,256]{3,2,0,1:T(8,128)(2,1)} async-done(((bf16[1,4,640,256]{3,2,0,1:T(8,128)(2,1)}), bf16[8,4,640,256]{3,2,0,1:T(8,128)(2,1)}) %all-gather.2.cloned.1.call-update) | async-done | bytes 10485776 | tf_op jit(solution)/shard_map/all_gather | solution.py:73
  188.9 14.6 %copy.11 = bf16[4,5120,256]{2,0,1:T(4,128)(2,1)} copy(bf16[4,5120,256]{2,1,0:T(8,128)(2,1)} %bitcast.15) | data formatting | bytes 20971520 | tf_op jit(solution)/shard_map/reshape | solution.py:73
  203.6 7.9 %gather_fusion.1 = bf16[1024,4,256]{2,1,0:T(4,128)(2,1)S(1)} fusion(bf16[4,5120,256]{2,0,1:T(4,128)(2,1)} %copy.11, s32[1024]{0:T(1024)S(1)} %broadcast_clamp_fusion), kind=kCustom, calls=%fused_computation.1 | custom fusion | bytes 4198400 | tf_op jit(solution)/shard_map/jit(_take)/gather | solution.py:75
  211.5 6.5 %select_bitcast_fusion = bf16[4,1024,256]{2,0,1:T(4,128)(2,1)S(1)} fusion(bf16[1024,4,256]{2,1,0:T(4,128)(2,1)S(1)} %gather_fusion.1, pred[1024]{0:T(1024)(128)(4,1)S(1)} %get-tuple-element.12, pred[1024]{0:T(1024)(128)(4,1)S(1)} %get-tuple-element.11), kind=kLoop, calls=%fused_computation.9 | loop fusion | flops 2097152 | bytes 4196352 | tf_op jit(solution)/shard_map/jit(_where)/select_n | solution.py:76
  217.9 0.5 slice_convert_fusion.1
  218.5 0.5 multiply_add_fusion
  219.0 2.2 maximum_reduce_fusion
  221.2 0.0 all-reduce.3.cloned.1.call-update
  221.3 31.7 %all-reduce.3.cloned.1.call-done = f32[512,256]{1,0:T(8,128)} async-done(((f32[512,256]{1,0:T(8,128)}), f32[512,256]{1,0:T(8,128)}) %all-reduce.3.cloned.1.call-update) | async-done | bytes 524304 | tf_op jit(solution)/shard_map/psum | solution.py:79
  253.0 1.9 broadcast_multiply_fusion
  (10 shorter events, 0.1 us)
Async XLA Ops:
  6.5 182.4 %all-gather.2.cloned.1.call-start = ((), (), s32[]{:S(2)}) async-start(), calls=%async_computation | async-start | bytes 11796480 | tf_op jit(solution)/shard_map/all_gather | solution.py:73
  11.3 1.7 slice-start
  33.9 1.9 copy-start
  33.9 8.6 %copy-start.1 = (s32[512,2]{0,1:T(2,128)S(1)}, s32[512,2]{0,1:T(2,128)}, u32[]{:S(2)}) copy-start(s32[512,2]{0,1:T(2,128)} %param.7) | copy-start | bytes 12292
  35.5 217.5 %all-reduce.3.cloned.1.call-start = ((), (), s32[]{:S(2)}) async-start(), calls=%async_computation.1 | async-start | bytes 1048576 | tf_op jit(solution)/shard_map/psum | solution.py:79
Sparse Core Ops, SparseCore 0:
  35.6 153.2 all-gather.1
  221.4 31.5 all-reduce.2
